TPU v7x, 32 devices: a whole 2x2x4 slice. The times are simulated.
32 devices in a mesh: kz: 4 (over x, core), en: 8 (over z, y).
Axes of the slice: x: 2, y: 2, z: 4, core: 2. Of those that a mesh axis runs over, the one named last changes fastest.
Arguments:
- green_blocks: float32 [4, 16, 2, 256, 256], P('kz', 'en'), may hold values from -6 to 6
- couplings: float32 [4, 8, 2, 256, 256], P('kz', 'en'), may hold values from -0.375 to 0.375
- owners: int32 [2], replicated, may hold values from 0 to 31
- momentum_shift: int32 [2], replicated, may hold values from -3 to 3
- energy_shift: int32 [2], replicated, may hold values from 1 to 7
Outputs:
- self_energy: float32 [4, 16, 2, 256, 256], P('kz', 'en')
Inputs may be any that keep to these rules, and one draw needn't show every extreme that they name: `owners`: flat device index of each mode's coupling block.
All inputs are finite; a program needn't handle non-finite values.
Results may differ from a plain program's by a relative error of at most 0.0001.
Values sent between devices are 32-bit elements; how exact they have to be, the bound alone decides.
No kernel may reach another device: no remote copies, remote signals or barrier semaphores. Data moves between devices by JAX's collectives and lax.ppermute only.
A program may use at most 64 MiB of HBM per device.

v0:
```python
import jax
import jax.numpy as jnp
from jax import lax
from jax.experimental import pallas as pl
from jax.experimental.pallas import tpu as pltpu
from jax.sharding import PartitionSpec as P


AXES = ("kz", "en")
MAX_SHIFT = 7
MAX_BRANCHES = 64


def sizes():
    return lax.axis_size("kz"), lax.axis_size("en")


def pairs_shift(momentum, energy):
    n_kz, n_en = sizes()
    return [
        (k * n_en + d, (k + momentum) % n_kz * n_en + d + energy)
        for k in range(n_kz)
        for d in range(n_en)
        if d + energy < n_en
    ]


def pairs_flip(kz_bits, en_bits):
    n_kz, n_en = sizes()
    return [(k * n_en + d, (k ^ kz_bits) * n_en + (d ^ en_bits)) for k in range(n_kz) for d in range(n_en)]


def flip(array, kz_bits, en_bits):
    return lax.ppermute(array, AXES, pairs_flip(kz_bits, en_bits))


def shift_blocks(blocks, momentum, energy):
    count = len(blocks)
    out = []
    for place in reversed(range(count)):
        source = (place - energy) % count
        steps = (energy - place + source) // count
        if momentum == 0 and steps == 0:
            out.append(blocks[source])
        else:
            out.append(lax.ppermute(blocks[source], AXES, pairs_shift(momentum, steps)))
    return tuple(reversed(out))


def move(blocks, momentum, energy, low, high, ride, operands):
    n_kz, _ = sizes()
    count = high - low + 1

    def branch(q, e):
        def run(held, ops):
            held, ops = ride(held, ops)
            return shift_blocks(held, q, e), ops

        return run

    if n_kz * count <= MAX_BRANCHES:
        branches = [branch(q, e) for q in range(n_kz) for e in range(low, high + 1)]
        return lax.switch(momentum * count + energy - low, branches, blocks, operands)
    blocks, more = lax.switch(energy - low, [branch(0, e) for e in range(low, high + 1)], blocks, operands)
    for bit in range((n_kz - 1).bit_length()):
        blocks = lax.cond(
            bit_of(momentum, bit) == 1,
            lambda held, bit=bit: shift_blocks(held, 1 << bit, 0),
            lambda held: held,
            blocks,
        )
    return blocks, more


def bit_of(number, bit):
    return lax.bitwise_and(lax.shift_right_logical(number, jnp.int32(bit)), jnp.int32(1))


def position():
    k, d = lax.axis_index("kz"), lax.axis_index("en")
    return bit_of(k, 0), 2 * bit_of(k, 1) + bit_of(d, 0)


def scatter_couplings(own, owners):
    core, chip = position()
    _, rows, _ = own.shape
    quarter = rows // 4
    n_en_bits = (sizes()[1] - 1).bit_length()
    theirs = flip(lax.dynamic_index_in_dim(own, 1 - core, 0, keepdims=False), 1, 0)
    mine = lax.dynamic_index_in_dim(own, core, 0, keepdims=False)

    def piece(which):
        here = lax.dynamic_slice_in_dim(mine, which * quarter, quarter, 0)
        there = lax.dynamic_slice_in_dim(theirs, which * quarter, quarter, 0)
        return jnp.stack([jnp.where(bit_of(owner, n_en_bits) == core, here, there) for owner in owners])

    far = {j: flip(piece(chip ^ j), j // 2 * 2, j % 2) for j in (3, 2, 1)}
    value = piece(chip)
    out = []
    for mode, owner in enumerate(owners):
        holder = (2 * bit_of(owner, n_en_bits + 1) + bit_of(owner, 0)) ^ chip
        chosen = value[mode]
        for j in (1, 2, 3):
            chosen = jnp.where(holder == j, far[j][mode], chosen)
        out.append(chosen)
    return jnp.stack(out)


def spread_bit(value, owners, axis, bit):
    here = bit_of(lax.axis_index(axis), bit)
    shift = 0 if axis == "en" else (sizes()[1] - 1).bit_length()
    other = flip(value, 0, 1 << bit) if axis == "en" else flip(value, 1 << bit, 0)
    return jnp.stack(
        [jnp.where(bit_of(owner, shift + bit) == here, value[mode], other[mode]) for mode, owner in enumerate(owners)]
    )


def dot(left, right):
    return jnp.dot(left, right, preferred_element_type=jnp.float32)


def dot_nt(left, right):
    return lax.dot_general(left, right, (((1,), (1,)), ((), ())), preferred_element_type=jnp.float32)


def split(value):
    high = value.astype(jnp.bfloat16)
    return high, (value - high.astype(jnp.float32)).astype(jnp.bfloat16)


def kernel(place, *refs):
    near, blocks, out = refs[:5], refs[5:9], refs[9]
    high, low, green_high, green_low = refs[10:]
    pieces = (near[:4], [near[4].at[j] for j in range(4)])
    core, chip = place[0], place[1]
    size = out.shape[-1]
    for mode in range(2):
        for half in range(2):
            for j in range(4):
                top, rest = split(pieces[half][j][place[2] ^ mode])
                high[mode, core ^ half, chip ^ j] = top
                low[mode, core ^ half, chip ^ j] = rest
    for mode in range(2):
        for local in range(2):
            for part in range(2):
                top, rest = split(blocks[mode * 2 + local][0, 0, part])
                green_high[mode * 2 + local, part] = top
                green_low[mode * 2 + local, part] = rest
    out[...] = jnp.zeros_like(out)

    def step(index, _):
        mode, local = index // 2, index % 2
        vrh, vih = (high[mode, part].reshape(size, size) for part in range(2))
        vrl, vil = (low[mode, part].reshape(size, size) for part in range(2))
        grh, gih = green_high[index, 0], green_high[index, 1]
        grl, gil = green_low[index, 0], green_low[index, 1]
        left = jnp.concatenate([vrh, vrh, vrl, vih, vih, vil], axis=1)
        real = dot(left, jnp.concatenate([grh, grl, grh, -gih, -gil, -gih], axis=0))
        imag = dot(left, jnp.concatenate([gih, gil, gih, grh, grl, grh], axis=0))
        rh, rl = split(real)
        ih, il = split(imag)
        right = jnp.concatenate([vrh, vrl, vrh, vih, vil, vih], axis=1)
        out[0, local, 0] += dot_nt(jnp.concatenate([rh, rh, rl, ih, ih, il], axis=1), right)
        out[0, local, 1] += dot_nt(jnp.concatenate([ih, ih, il, -rh, -rh, -rl], axis=1), right)
        return 0

    lax.fori_loop(0, 4, step, 0)


def sandwich_sum(place, pieces, blocks, shape):
    size = shape[-1]
    vmem = pl.BlockSpec(memory_space=pltpu.VMEM)
    return pl.pallas_call(
        kernel,
        out_shape=jax.ShapeDtypeStruct(shape, jnp.float32),
        in_specs=[pl.BlockSpec(memory_space=pltpu.SMEM)] + [vmem] * 9,
        out_specs=vmem,
        scratch_shapes=[pltpu.VMEM((2, 2, 4, size // 4, size), jnp.bfloat16)] * 2
        + [pltpu.VMEM((4, 2, size, size), jnp.bfloat16)] * 2,
        cost_estimate=pl.CostEstimate(flops=192 * size**3, bytes_accessed=16 * size * size * 4, transcendentals=0),
        name="sandwich_sum",
    )(place, *pieces, *blocks)


def shards(green_blocks, couplings, owners, momentum_shift, energy_shift):
    n_kz, n_en = sizes()
    local = green_blocks.shape[1]
    assert n_kz & (n_kz - 1) == 0 and n_en & (n_en - 1) == 0
    swap = energy_shift[0] > energy_shift[1]
    e_first, e_second = jnp.minimum(energy_shift[0], energy_shift[1]), jnp.maximum(energy_shift[0], energy_shift[1])
    q_first = jnp.where(swap, momentum_shift[1], momentum_shift[0])
    q_more = jnp.where(swap, momentum_shift[0], momentum_shift[1]) - q_first
    q_first, q_more = q_first & (n_kz - 1), q_more & (n_kz - 1)
    e_more = e_second - e_first
    owner = (owners[0], owners[1])
    blocks = tuple(green_blocks[:, i : i + 1] for i in range(local))
    en_rest = [("en", bit) for bit in range(1, (n_en - 1).bit_length())]
    rest = en_rest + [("kz", bit) for bit in range(2, (n_kz - 1).bit_length())]

    value = scatter_couplings(couplings[0, 0], owner)

    def early(held, ops):
        value, owner = ops
        for step, (axis, bit) in enumerate(rest):
            value = spread_bit(value, owner, axis, bit)
            if step == 0:
                last, value = lax.optimization_barrier((held[-1], value))
                held = held[:-1] + (last,)
        return held, value

    def late(held, value):
        pieces = [value] + [None] * 3
        for j in (3, 2, 1):
            pieces[j] = flip(value, j // 2 * 2, j % 2)
        return held, tuple(pieces) + (flip(jnp.stack(pieces), 1, 0),)

    blocks, q_more, e_more, q_first, e_first = lax.optimization_barrier((blocks, q_more, e_more, q_first, e_first))
    near, value = move(blocks, q_first, e_first, 1, MAX_SHIFT, early, (value, owner))
    far, pieces = move(near, q_more, e_more, 0, MAX_SHIFT - 1, late, value)
    place = jnp.stack([*position(), swap.astype(jnp.int32)])
    return sandwich_sum(place, pieces, near + far, green_blocks.shape)


def solution(mesh):
    in_specs = (P("kz", "en", None, None, None), P("kz", "en", None, None, None), P(), P(), P())
    out_specs = P("kz", "en", None, None, None)
    return jax.shard_map(shards, mesh=mesh, in_specs=in_specs, out_specs=out_specs, check_vma=False)
```

profile of v0, /device:TPU:24, one launch (start us, length us, event | category | flops | bytes accessed | tf_op | source)
XLA Modules:
  0.0 94.4 jit_solution(12065740962732112983)
XLA Ops:
  0.0 1.0 %dynamic-slice_bitcast_fusion = f32[256,256]{1,0:T(8,128)S(1)} fusion(f32[1,1,2,256,256]{4,3,2,1,0:T(8,128)} %param.62, s32[]{:T(128)S(6)} %select_n.852), kind=kLoop, calls=%fused_computation.308 | loop fusion | bytes 524292 | tf_op jit(solution)/shard_map/jit(dynamic_index_in_dim)/squeeze | solution.py:89
  1.1 0.6 copy-done.1
  1.7 0.6 fusion.125
  3.6 0.6 copy-done.2
  4.2 0.6 fusion.126
  4.8 1.3 %fusion.124 = (f32[1,1,2,256,256]{4,3,2,1,0:T(8,128)S(1)}, f32[1,1,2,256,256]{4,3,2,1,0:T(8,128)S(1)}) fusion(f32[1,2,2,256,256]{4,3,2,1,0:T(8,128)} %param.61), kind=kLoop, calls=%fused_computation.340 | loop fusion | bytes 2097152 | tf_op jit(solution)/shard_map/slice | solution.py:196
  6.2 1.6 %collective-permute-start.279 = (f32[2,64,256]{2,1,0:T(8,128)S(1)}, f32[2,64,256]{2,1,0:T(8,128)S(1)}, u32[]{:S(2)}, u32[]{:S(2)}) collective-permute-start(f32[2,64,256]{2,1,0:T(8,128)S(1)} %pad_maximum_fusion.86), channel_id=1, source_target_pairs={{0,1},{1,0},{2,3},{3,2},{4,5},{5,4},{6,7},{7,6},{8,9},{9,8},{10,11... | collective-permute-start | bytes 393224 | tf_op jit(solution)/shard_map/ppermute | solution.py:34
  7.8 1.6 %collective-permute-start.278 = (f32[2,64,256]{2,1,0:T(8,128)S(1)}, f32[2,64,256]{2,1,0:T(8,128)S(1)}, u32[]{:S(2)}, u32[]{:S(2)}) collective-permute-start(f32[2,64,256]{2,1,0:T(8,128)S(1)} %pad_maximum_fusion.85), channel_id=1, source_target_pairs={{0,16},{1,17},{2,18},{3,19},{4,20},{5,21},{6,22},{7,23},{8,24},{9,... | collective-permute-start | bytes 393224 | tf_op jit(solution)/shard_map/ppermute | solution.py:34
  9.4 0.5 collective-permute-start.277
  10.0 0.1 copy-done.3
  10.1 0.6 fusion.127
  19.3 0.6 pad_add_fusion.place
  19.9 34.8 %conditional.2 = (f32[1,1,2,256,256]{4,3,2,1,0:T(8,128)}, f32[1,1,2,256,256]{4,3,2,1,0:T(8,128)}, f32[2,64,256]{2,1,0:T(8,128)S(1)}) conditional(s32[]{:T(128)} %clamp.46, (s32[]{:T(128)}, f32[2,64,256]{2,1,0:T(8,128)S(1)}, f32[64,256]{1,0:T(8,128)S(1)}, s32[]{:T(128)}, f32[64,256]{1,0:T(8,128)S(1)}, ...), branch_computations={%region_0.1_spmd, %region_1.2_spmd, %region_2.3_spmd, %region_3.4_... | conditional | flops 131090 | bytes 6553988 | solution.py:63
  20.0 0.5 collective-permute-start.96
  20.5 1.3 %collective-permute-start.95 = (f32[1,1,2,256,256]{4,3,2,1,0:T(8,128)S(1)}, f32[1,1,2,256,256]{4,3,2,1,0:T(8,128)}, u32[]{:S(2)}, u32[]{:S(2)}) collective-permute-start(f32[1,1,2,256,256]{4,3,2,1,0:T(8,128)S(1)} %get-tuple-element.781), channel_id=1, source_target_pairs={{0,26},{1,27},{2,28},{3,29},{4,30},{5,31},{8,2},{9,3},{10,4},{11,5... | collective-permute-start | bytes 1572872 | tf_op jit(solution)/shard_map/cond/branch_24_fun/ppermute | solution.py:46
  23.0 2.3 %collective-permute-done.96 = f32[2,64,256]{2,1,0:T(8,128)S(1)} collective-permute-done((f32[2,64,256]{2,1,0:T(8,128)S(1)}, f32[2,64,256]{2,1,0:T(8,128)S(1)}, u32[]{:S(2)}, u32[]{:S(2)}) %collective-permute-start.96) | collective-permute-done | bytes 131104 | tf_op jit(solution)/shard_map/cond/branch_24_fun/ppermute | solution.py:34
  25.4 1.3 %collective-permute-start.97 = (f32[1,1,2,256,256]{4,3,2,1,0:T(8,128)S(1)}, f32[1,1,2,256,256]{4,3,2,1,0:T(8,128)}, u32[]{:S(2)}, u32[]{:S(2)}) collective-permute-start(f32[1,1,2,256,256]{4,3,2,1,0:T(8,128)S(1)} %get-tuple-element.788), channel_id=1, source_target_pairs={{0,26},{1,27},{2,28},{3,29},{4,30},{5,31},{8,2},{9,3},{10,4},{11,5... | collective-permute-start | bytes 1572872 | tf_op jit(solution)/shard_map/cond/branch_24_fun/ppermute | solution.py:46
  26.7 3.0 %collective-permute-start.98 = (f32[2,64,256]{2,1,0:T(8,128)S(1)}, f32[2,64,256]{2,1,0:T(8,128)S(1)}, u32[]{:S(2)}, u32[]{:S(2)}) collective-permute-start(f32[2,64,256]{2,1,0:T(8,128)S(1)} %pad_maximum_fusion.48), channel_id=1, source_target_pairs={{0,4},{1,5},{2,6},{3,7},{4,0},{5,1},{6,2},{7,3},{8,12},{9,13},{10,... | collective-permute-start | bytes 393224 | tf_op jit(solution)/shard_map/cond/branch_24_fun/ppermute | solution.py:34
  30.9 23.6 %collective-permute-done.98 = f32[2,64,256]{2,1,0:T(8,128)S(1)} collective-permute-done((f32[2,64,256]{2,1,0:T(8,128)S(1)}, f32[2,64,256]{2,1,0:T(8,128)S(1)}, u32[]{:S(2)}, u32[]{:S(2)}) %collective-permute-start.98) | collective-permute-done | bytes 131104 | tf_op jit(solution)/shard_map/cond/branch_24_fun/ppermute | solution.py:34
  54.7 32.2 %conditional.3 = (f32[1,1,2,256,256]{4,3,2,1,0:T(8,128)}, f32[1,1,2,256,256]{4,3,2,1,0:T(8,128)}, f32[2,64,256]{2,1,0:T(8,128)}, f32[2,64,256]{2,1,0:T(8,128)}, ...) conditional(s32[]{:T(128)} %clamp.47, (f32[2,64,256]{2,1,0:T(8,128)S(1)}, ...), branch_computations={%region_28.29_spmd, %region_29.30_spmd, %region_30.31_spmd, %regio... | conditional | flops 393216 | bytes 8913184 | solution.py:63
  54.8 1.4 %collective-permute-start.250 = (f32[2,64,256]{2,1,0:T(8,128)S(1)}, f32[2,64,256]{2,1,0:T(8,128)}, u32[]{:S(2)}, u32[]{:S(2)}) collective-permute-start(f32[2,64,256]{2,1,0:T(8,128)S(1)} %get-tuple-element.888), channel_id=1, source_target_pairs={{0,17},{1,16},{2,19},{3,18},{4,21},{5,20},{6,23},{7,22},{8,25},{9,... | collective-permute-start | bytes 393224 | tf_op jit(solution)/shard_map/cond/branch_23_fun/ppermute | solution.py:34
  56.2 1.6 %collective-permute-start.249 = (f32[2,64,256]{2,1,0:T(8,128)S(1)}, f32[2,64,256]{2,1,0:T(8,128)}, u32[]{:S(2)}, u32[]{:S(2)}) collective-permute-start(f32[2,64,256]{2,1,0:T(8,128)S(1)} %get-tuple-element.888), channel_id=1, source_target_pairs={{0,16},{1,17},{2,18},{3,19},{4,20},{5,21},{6,22},{7,23},{8,24},{9,... | collective-permute-start | bytes 393224 | tf_op jit(solution)/shard_map/cond/branch_23_fun/ppermute | solution.py:34
  57.8 0.6 collective-permute-start.248
  58.4 2.3 %collective-permute-start.246 = (f32[1,1,2,256,256]{4,3,2,1,0:T(8,128)}, f32[1,1,2,256,256]{4,3,2,1,0:T(8,128)}, u32[]{:S(2)}, u32[]{:S(2)}) collective-permute-start(f32[1,1,2,256,256]{4,3,2,1,0:T(8,128)} %get-tuple-element.886), channel_id=1, source_target_pairs={{0,25},{1,26},{2,27},{3,28},{4,29},{5,30},{6,31},{8,1},{9,2},{10,3... | collective-permute-start | bytes 1572872 | tf_op jit(solution)/shard_map/cond/branch_23_fun/ppermute | solution.py:46
  60.7 1.9 %collective-permute-start.247 = (f32[1,1,2,256,256]{4,3,2,1,0:T(8,128)}, f32[1,1,2,256,256]{4,3,2,1,0:T(8,128)}, u32[]{:S(2)}, u32[]{:S(2)}) collective-permute-start(f32[1,1,2,256,256]{4,3,2,1,0:T(8,128)} %get-tuple-element.887), channel_id=1, source_target_pairs={{0,25},{1,26},{2,27},{3,28},{4,29},{5,30},{6,31},{8,1},{9,2},{10,3... | collective-permute-start | bytes 1572872 | tf_op jit(solution)/shard_map/cond/branch_23_fun/ppermute | solution.py:46
  62.6 1.1 %collective-permute-done.249 = f32[2,64,256]{2,1,0:T(8,128)} collective-permute-done((f32[2,64,256]{2,1,0:T(8,128)S(1)}, f32[2,64,256]{2,1,0:T(8,128)}, u32[]{:S(2)}, u32[]{:S(2)}) %collective-permute-start.249) | collective-permute-done | bytes 131104 | tf_op jit(solution)/shard_map/cond/branch_23_fun/ppermute | solution.py:34
  63.7 0.1 collective-permute-done.248
  63.9 1.1 %pad_maximum_fusion.79 = f32[4,2,64,256]{3,2,1,0:T(8,128)S(1)} fusion(f32[1,2,64,256]{3,2,1,0:T(8,128)} %bitcast.207, f32[1,2,64,256]{3,2,1,0:T(8,128)} %bitcast.206, f32[1,2,64,256]{3,2,1,0:T(8,128)} %bitcast.205, f32[1,2,64,256]{3,2,1,0:T(8,128)S(1)} %bitcast.667), kind=kLoop, calls=%fused_computation.303 | loop fusion | flops 393216 | bytes 1048576 | tf_op jit(solution)/shard_map/cond/branch_23_fun/stack | solution.py:215
  64.9 0.1 collective-permute-start.251
  65.0 10.9 %collective-permute-done.246 = f32[1,1,2,256,256]{4,3,2,1,0:T(8,128)} collective-permute-done((f32[1,1,2,256,256]{4,3,2,1,0:T(8,128)}, f32[1,1,2,256,256]{4,3,2,1,0:T(8,128)}, u32[]{:S(2)}, u32[]{:S(2)}) %collective-permute-start.246) | collective-permute-done | bytes 524320 | tf_op jit(solution)/shard_map/cond/branch_23_fun/ppermute | solution.py:46
  76.0 11.0 %collective-permute-done.247 = f32[1,1,2,256,256]{4,3,2,1,0:T(8,128)} collective-permute-done((f32[1,1,2,256,256]{4,3,2,1,0:T(8,128)}, f32[1,1,2,256,256]{4,3,2,1,0:T(8,128)}, u32[]{:S(2)}, u32[]{:S(2)}) %collective-permute-start.247) | collective-permute-done | bytes 524320 | tf_op jit(solution)/shard_map/cond/branch_23_fun/ppermute | solution.py:46
  86.9 7.5 %sandwich_sum.1 = f32[1,2,2,256,256]{4,3,2,1,0:T(8,128)} custom-call(s32[3]{0:T(128)} %pad_add_fusion.place, f32[2,64,256]{2,1,0:T(8,128)S(1)} %get-tuple-element.920.refs_0_, f32[2,64,256]{2,1,0:T(8,128)} %get-tuple-element.925.refs_1_, f32[2,64,256]{2,1,0:T(8,128)} %get-tuple-element.926.refs_2_, f32[2,64,256]{2,1,0:T(8,128)} %get-tuple-element.927.refs_3_, ...), custom_call_target="tpu_custom_call" | custom-call | flops 3221225472 | bytes 4194304 | tf_op jit(solution)/shard_map/sandwich_sum/pallas_call | solution.py:173
  (24 shorter events, 0.3 us)
Async XLA Ops:
  1.0 5.2 %collective-permute-start.276 = (f32[256,256]{1,0:T(8,128)S(1)}, f32[256,256]{1,0:T(8,128)S(1)}, u32[]{:S(2)}, u32[]{:S(2)}) collective-permute-start(f32[256,256]{1,0:T(8,128)S(1)} %dynamic-slice_bitcast_fusion), channel_id=1, source_target_pairs={{0,8},{1,9},{2,10},{3,11},{4,12},{5,13},{6,14},{7,15},{8,0},{9,1},... | collective-permute-start | bytes 786440 | tf_op jit(solution)/shard_map/ppermute | solution.py:34
  1.1 0.7 copy-start.1
  3.6 0.7 copy-start.2
  4.8 1.4 %copy-start = (f32[1,1,2,256,256]{4,3,2,1,0:T(8,128)S(1)}, f32[1,1,2,256,256]{4,3,2,1,0:T(8,128)}, u32[]{:S(2)}) copy-start(f32[1,1,2,256,256]{4,3,2,1,0:T(8,128)} %param.62) | copy-start | bytes 1572868
  6.2 13.6 %collective-permute-start.279 = (f32[2,64,256]{2,1,0:T(8,128)S(1)}, f32[2,64,256]{2,1,0:T(8,128)S(1)}, u32[]{:S(2)}, u32[]{:S(2)}) collective-permute-start(f32[2,64,256]{2,1,0:T(8,128)S(1)} %pad_maximum_fusion.86), channel_id=1, source_target_pairs={{0,1},{1,0},{2,3},{3,2},{4,5},{5,4},{6,7},{7,6},{8,9},{9,8},{10,11... | collective-permute-start | bytes 393224 | tf_op jit(solution)/shard_map/ppermute | solution.py:34
  7.8 12.0 %collective-permute-start.278 = (f32[2,64,256]{2,1,0:T(8,128)S(1)}, f32[2,64,256]{2,1,0:T(8,128)S(1)}, u32[]{:S(2)}, u32[]{:S(2)}) collective-permute-start(f32[2,64,256]{2,1,0:T(8,128)S(1)} %pad_maximum_fusion.85), channel_id=1, source_target_pairs={{0,16},{1,17},{2,18},{3,19},{4,20},{5,21},{6,22},{7,23},{8,24},{9,... | collective-permute-start | bytes 393224 | tf_op jit(solution)/shard_map/ppermute | solution.py:34
  9.4 0.7 copy-start.3
  9.4 10.4 %collective-permute-start.277 = (f32[2,64,256]{2,1,0:T(8,128)S(1)}, f32[2,64,256]{2,1,0:T(8,128)S(1)}, u32[]{:S(2)}, u32[]{:S(2)}) collective-permute-start(f32[2,64,256]{2,1,0:T(8,128)S(1)} %pad_maximum_fusion.84), channel_id=1, source_target_pairs={{0,17},{1,16},{2,19},{3,18},{4,21},{5,20},{6,23},{7,22},{8,25},{9,... | collective-permute-start | bytes 393224 | tf_op jit(solution)/shard_map/ppermute | solution.py:34
  20.0 5.4 %collective-permute-start.96 = (f32[2,64,256]{2,1,0:T(8,128)S(1)}, f32[2,64,256]{2,1,0:T(8,128)S(1)}, u32[]{:S(2)}, u32[]{:S(2)}) collective-permute-start(f32[2,64,256]{2,1,0:T(8,128)S(1)} %get-tuple-element.785), channel_id=1, source_target_pairs={{0,2},{1,3},{2,0},{3,1},{4,6},{5,7},{6,4},{7,5},{8,10},{9,11},{10,... | collective-permute-start | bytes 393224 | tf_op jit(solution)/shard_map/cond/branch_24_fun/ppermute | solution.py:34
  20.5 34.0 %collective-permute-start.95 = (f32[1,1,2,256,256]{4,3,2,1,0:T(8,128)S(1)}, f32[1,1,2,256,256]{4,3,2,1,0:T(8,128)}, u32[]{:S(2)}, u32[]{:S(2)}) collective-permute-start(f32[1,1,2,256,256]{4,3,2,1,0:T(8,128)S(1)} %get-tuple-element.781), channel_id=1, source_target_pairs={{0,26},{1,27},{2,28},{3,29},{4,30},{5,31},{8,2},{9,3},{10,4},{11,5... | collective-permute-start | bytes 1572872 | tf_op jit(solution)/shard_map/cond/branch_24_fun/ppermute | solution.py:46
  25.4 29.1 %collective-permute-start.97 = (f32[1,1,2,256,256]{4,3,2,1,0:T(8,128)S(1)}, f32[1,1,2,256,256]{4,3,2,1,0:T(8,128)}, u32[]{:S(2)}, u32[]{:S(2)}) collective-permute-start(f32[1,1,2,256,256]{4,3,2,1,0:T(8,128)S(1)} %get-tuple-element.788), channel_id=1, source_target_pairs={{0,26},{1,27},{2,28},{3,29},{4,30},{5,31},{8,2},{9,3},{10,4},{11,5... | collective-permute-start | bytes 1572872 | tf_op jit(solution)/shard_map/cond/branch_24_fun/ppermute | solution.py:46
  26.7 27.8 %collective-permute-start.98 = (f32[2,64,256]{2,1,0:T(8,128)S(1)}, f32[2,64,256]{2,1,0:T(8,128)S(1)}, u32[]{:S(2)}, u32[]{:S(2)}) collective-permute-start(f32[2,64,256]{2,1,0:T(8,128)S(1)} %pad_maximum_fusion.48), channel_id=1, source_target_pairs={{0,4},{1,5},{2,6},{3,7},{4,0},{5,1},{6,2},{7,3},{8,12},{9,13},{10,... | collective-permute-start | bytes 393224 | tf_op jit(solution)/shard_map/cond/branch_24_fun/ppermute | solution.py:34
  54.8 7.8 %collective-permute-start.250 = (f32[2,64,256]{2,1,0:T(8,128)S(1)}, f32[2,64,256]{2,1,0:T(8,128)}, u32[]{:S(2)}, u32[]{:S(2)}) collective-permute-start(f32[2,64,256]{2,1,0:T(8,128)S(1)} %get-tuple-element.888), channel_id=1, source_target_pairs={{0,17},{1,16},{2,19},{3,18},{4,21},{5,20},{6,23},{7,22},{8,25},{9,... | collective-permute-start | bytes 393224 | tf_op jit(solution)/shard_map/cond/branch_23_fun/ppermute | solution.py:34
  56.2 7.5 %collective-permute-start.249 = (f32[2,64,256]{2,1,0:T(8,128)S(1)}, f32[2,64,256]{2,1,0:T(8,128)}, u32[]{:S(2)}, u32[]{:S(2)}) collective-permute-start(f32[2,64,256]{2,1,0:T(8,128)S(1)} %get-tuple-element.888), channel_id=1, source_target_pairs={{0,16},{1,17},{2,18},{3,19},{4,20},{5,21},{6,22},{7,23},{8,24},{9,... | collective-permute-start | bytes 393224 | tf_op jit(solution)/shard_map/cond/branch_23_fun/ppermute | solution.py:34
  57.8 6.1 %collective-permute-start.248 = (f32[2,64,256]{2,1,0:T(8,128)S(1)}, f32[2,64,256]{2,1,0:T(8,128)}, u32[]{:S(2)}, u32[]{:S(2)}) collective-permute-start(f32[2,64,256]{2,1,0:T(8,128)S(1)} %get-tuple-element.888), channel_id=1, source_target_pairs={{0,1},{1,0},{2,3},{3,2},{4,5},{5,4},{6,7},{7,6},{8,9},{9,8},{10,11... | collective-permute-start | bytes 393224 | tf_op jit(solution)/shard_map/cond/branch_23_fun/ppermute | solution.py:34
  58.4 17.6 %collective-permute-start.246 = (f32[1,1,2,256,256]{4,3,2,1,0:T(8,128)}, f32[1,1,2,256,256]{4,3,2,1,0:T(8,128)}, u32[]{:S(2)}, u32[]{:S(2)}) collective-permute-start(f32[1,1,2,256,256]{4,3,2,1,0:T(8,128)} %get-tuple-element.886), channel_id=1, source_target_pairs={{0,25},{1,26},{2,27},{3,28},{4,29},{5,30},{6,31},{8,1},{9,2},{10,3... | collective-permute-start | bytes 1572872 | tf_op jit(solution)/shard_map/cond/branch_23_fun/ppermute | solution.py:46
  60.7 26.2 %collective-permute-start.247 = (f32[1,1,2,256,256]{4,3,2,1,0:T(8,128)}, f32[1,1,2,256,256]{4,3,2,1,0:T(8,128)}, u32[]{:S(2)}, u32[]{:S(2)}) collective-permute-start(f32[1,1,2,256,256]{4,3,2,1,0:T(8,128)} %get-tuple-element.887), channel_id=1, source_target_pairs={{0,25},{1,26},{2,27},{3,28},{4,29},{5,30},{6,31},{8,1},{9,2},{10,3... | collective-permute-start | bytes 1572872 | tf_op jit(solution)/shard_map/cond/branch_23_fun/ppermute | solution.py:46
  64.9 22.0 %collective-permute-start.251 = (f32[4,2,64,256]{3,2,1,0:T(8,128)S(1)}, f32[4,2,64,256]{3,2,1,0:T(8,128)}, u32[]{:S(2)}, u32[]{:S(2)}) collective-permute-start(f32[4,2,64,256]{3,2,1,0:T(8,128)S(1)} %pad_maximum_fusion.79), channel_id=1, source_target_pairs={{0,8},{1,9},{2,10},{3,11},{4,12},{5,13},{6,14},{7,15},{8,0},{9,1},... | collective-permute-start | bytes 1572872 | tf_op jit(solution)/shard_map/cond/branch_23_fun/ppermute | solution.py:34
where the time goes:
time: 94.9 us; the launch traced here: 94.4 us
  waiting for transfers between devices  49.1 us (52%)
  starting transfers between devices  17.7 us (19%)
  between operations  10 us (11%)
  Pallas kernels  7.51 us (8%)
  local copies, waits for them, and re-layouts  5.46 us (6%)
  loops' own time  2.82 us (3%)
  other arithmetic  1.85 us (2%)
    ppermute x10, waiting for transfers between devices, flip(): return lax.ppermute(array, AXES, pairs_flip(kz_bits, en_bits))  27.2 us
    ppermute x4, waiting for transfers between devices, shift_blocks(): out.append(lax.ppermute(blocks[source], AXES, pairs_shift(momentum, steps)))  21.9 us
    ppermute x10, starting transfers between devices, flip(): return lax.ppermute(array, AXES, pairs_flip(kz_bits, en_bits))  10.9 us
    pallas_call x1, Pallas kernels, sandwich_sum(): pl.pallas_call(kernel, out_shape=jax.ShapeDtypeStruct(shape, jnp.float32)...  7.51 us
    ppermute x4, starting transfers between devices, shift_blocks(): out.append(lax.ppermute(blocks[source], AXES, pairs_shift(momentum, steps)))  6.81 us
    another operation x2, loops' own time, move(): lax.switch(momentum * count + energy - low, branches, blocks, operands)  2.82 us
  transfers between devices with their start and end apart: 14, of which 6 were waited for; matrix products, arithmetic and copies ran while one was open for 5% of the time, Pallas kernels for 0%

commit v1 on v0

v1 whole, which is shorter than its diff:
```python
import jax
import jax.numpy as jnp
from jax import lax
from jax.experimental import pallas as pl
from jax.experimental.pallas import tpu as pltpu
from jax.sharding import PartitionSpec as P


AXES = ("kz", "en")
MAX_SHIFT = 7
MAX_BRANCHES = 64


def sizes():
    return lax.axis_size("kz"), lax.axis_size("en")


def pairs_shift(momentum, energy):
    n_kz, n_en = sizes()
    return [
        (k * n_en + d, (k + momentum) % n_kz * n_en + d + energy)
        for k in range(n_kz)
        for d in range(n_en)
        if d + energy < n_en
    ]


def pairs_flip(kz_bits, en_bits):
    n_kz, n_en = sizes()
    return [(k * n_en + d, (k ^ kz_bits) * n_en + (d ^ en_bits)) for k in range(n_kz) for d in range(n_en)]


def flip(array, kz_bits, en_bits):
    return lax.ppermute(array, AXES, pairs_flip(kz_bits, en_bits))


def shift_blocks(blocks, momentum, energy):
    count = len(blocks)
    out = []
    for place in reversed(range(count)):
        source = (place - energy) % count
        steps = (energy - place + source) // count
        if momentum == 0 and steps == 0:
            out.append(blocks[source])
        else:
            out.append(lax.ppermute(blocks[source], AXES, pairs_shift(momentum, steps)))
    return tuple(reversed(out))


def move(blocks, index, low, ride, operands):
    n_kz, _ = sizes()

    def branch(q, e):
        def run(held, ops):
            held, ops = ride(held, ops)
            return shift_blocks(held, q, e + low), ops

        return run

    if n_kz * MAX_SHIFT <= MAX_BRANCHES:
        branches = [branch(q, e) for q in range(n_kz) for e in range(MAX_SHIFT)]
        return lax.switch(index, branches, blocks, operands)
    momentum = index // MAX_SHIFT
    blocks, more = lax.switch(index - momentum * MAX_SHIFT, [branch(0, e) for e in range(MAX_SHIFT)], blocks, operands)
    for bit in range((n_kz - 1).bit_length()):
        blocks = lax.cond(
            bit_of(momentum, bit) == 1,
            lambda held, bit=bit: shift_blocks(held, 1 << bit, 0),
            lambda held: held,
            blocks,
        )
    return blocks, more


def bit_of(number, bit):
    return (number >> bit) & 1


def bits_of(numbers, bit, value):
    return (bit_of(numbers, bit) == value)[:, None, None]


def position():
    k, d = lax.axis_index("kz"), lax.axis_index("en")
    return bit_of(k, 0), 2 * bit_of(k, 1) + bit_of(d, 0)


def part_of_both_cores(own):
    core, _ = position()
    theirs = flip(lax.dynamic_index_in_dim(own, 1 - core, 0, keepdims=False), 1, 0)
    return lax.dynamic_index_in_dim(own, core, 0, keepdims=False), theirs


def cut_couplings(mine, theirs, owners):
    core, chip = position()
    quarter = mine.shape[0] // 4
    from_core = bits_of(owners, (sizes()[1] - 1).bit_length(), core)

    def piece(which):
        here = lax.dynamic_slice_in_dim(mine, which * quarter, quarter, 0)
        there = lax.dynamic_slice_in_dim(theirs, which * quarter, quarter, 0)
        return jnp.where(from_core, here[None], there[None])

    return tuple(piece(chip ^ j) for j in range(4))


def scatter_couplings(pieces, owners):
    _, chip = position()
    far = {j: flip(pieces[j], j // 2 * 2, j % 2) for j in (3, 2, 1)}
    holder = ((2 * bit_of(owners, (sizes()[1] - 1).bit_length() + 1) + bit_of(owners, 0)) ^ chip)[:, None, None]
    value = pieces[0]
    for j in (1, 2, 3):
        value = jnp.where(holder == j, far[j], value)
    return value


def send_bit(value, axis, bit):
    return flip(value, 0, 1 << bit) if axis == "en" else flip(value, 1 << bit, 0)


def keep_bit(value, other, owners, axis, bit):
    shift = 0 if axis == "en" else (sizes()[1] - 1).bit_length()
    return jnp.where(bits_of(owners, shift + bit, bit_of(lax.axis_index(axis), bit)), value, other)


def dot(left, right):
    return jnp.dot(left, right, preferred_element_type=jnp.float32)


def dot_nt(left, right):
    return lax.dot_general(left, right, (((1,), (1,)), ((), ())), preferred_element_type=jnp.float32)


def split(value):
    high = value.astype(jnp.bfloat16)
    return high, (value - high.astype(jnp.float32)).astype(jnp.bfloat16)


def kernel(energy, *refs):
    near, blocks, out = refs[:5], refs[5:9], refs[9]
    coupling, green, sums, cut, sems, block_sems, out_sems = refs[10:]
    core, chip = position()
    swap = (energy[0] > energy[1]).astype(jnp.int32)
    quarter, size = coupling.shape[-2:]
    loads = [pltpu.make_async_copy(near[j], coupling.at[0, j], sems.at[j]) for j in range(4)]
    loads.append(pltpu.make_async_copy(near[4], coupling.at[1], sems.at[4]))
    for load in loads:
        load.start()
    for local in range(2):
        for mode in range(2):
            place = local * 2 + mode
            pltpu.make_async_copy(blocks[mode * 2 + local].at[0, 0], green.at[place], block_sems.at[place]).start()
    sums[...] = jnp.zeros_like(sums)
    for load in loads:
        load.wait()
    for mode in range(2):
        for j in range(4):
            rows = pl.ds(pl.multiple_of((chip ^ j) * quarter, quarter), quarter)
            real = coupling[core, j, swap ^ mode]
            imag = coupling[1 - core, j, swap ^ mode]
            for which, value in enumerate((real, imag, real + imag)):
                top, rest = split(value)
                cut[mode, which, rows, 0:size] = top
                cut[mode, which, rows, size : 2 * size] = top
                cut[mode, which, rows, 2 * size : 3 * size] = rest

    def left(mode, which, value):
        top, rest = split(value)
        return dot(cut[mode, which], jnp.concatenate([top, rest, top], axis=0))

    def right(mode, which, value):
        top, rest = split(value)
        return dot_nt(jnp.concatenate([top, rest, top], axis=1), cut[mode, which])

    def step(place, _):
        local, mode = place // 2, place % 2
        pltpu.make_async_copy(blocks[0].at[0, 0], green.at[place], block_sems.at[place]).wait()
        real, imag = green[place, 0], green[place, 1]
        first = left(mode, 0, real)
        second = left(mode, 1, imag)
        both = left(mode, 2, real + imag)
        real, imag = first - second, both - first - second
        first = right(mode, 0, real)
        second = right(mode, 1, imag)
        sums[local, 0] += first + second
        sums[local, 1] += first - second
        sums[local, 1] += right(mode, 2, imag - real)

        @pl.when(mode == 1)
        def _():
            pltpu.make_async_copy(sums.at[local], out.at[0, local], out_sems.at[local]).start()

        return 0

    lax.fori_loop(0, 4, step, 0)
    for local in range(2):
        pltpu.make_async_copy(sums.at[local], out.at[0, local], out_sems.at[local]).wait()


def sandwich_sum(energy, pieces, blocks, shape):
    size = shape[-1]
    anywhere = pl.BlockSpec(memory_space=pl.ANY)
    return pl.pallas_call(
        kernel,
        out_shape=jax.ShapeDtypeStruct(shape, jnp.float32),
        in_specs=[pl.BlockSpec(memory_space=pltpu.SMEM)] + [anywhere] * 9,
        out_specs=anywhere,
        scratch_shapes=[
            pltpu.VMEM((2, 4, 2, size // 4, size), jnp.float32),
            pltpu.VMEM((4, 2, size, size), jnp.float32),
            pltpu.VMEM((2, 2, size, size), jnp.float32),
            pltpu.VMEM((2, 3, size, 3 * size), jnp.bfloat16),
            pltpu.SemaphoreType.DMA((5,)),
            pltpu.SemaphoreType.DMA((4,)),
            pltpu.SemaphoreType.DMA((2,)),
        ],
        cost_estimate=pl.CostEstimate(flops=144 * size**3, bytes_accessed=16 * size * size * 4, transcendentals=0),
        name="sandwich_sum",
    )(energy, *pieces, *blocks)


def shards(green_blocks, couplings, owners, momentum_shift, energy_shift):
    n_kz, n_en = sizes()
    local = green_blocks.shape[1]
    pieces = cut_couplings(*part_of_both_cores(couplings[0, 0]), owners)
    pieces, green_blocks = lax.optimization_barrier((pieces, green_blocks))
    value = scatter_couplings(pieces, owners)
    assert n_kz & (n_kz - 1) == 0 and n_en & (n_en - 1) == 0
    count = MAX_SHIFT
    energy, momentum = energy_shift, momentum_shift
    energy_other, momentum_other = energy[::-1], momentum[::-1]
    low, high = jnp.minimum(energy, energy_other), jnp.maximum(energy, energy_other)
    first = jnp.where(energy > energy_other, momentum_other, momentum)
    more = jnp.where(energy_other > energy, momentum_other - momentum, momentum - momentum_other)
    lead = jnp.arange(2) == 0
    steps = jnp.where(lead, first, more) & (n_kz - 1)
    rise = jnp.where(lead, low - 1, high - low)
    index = steps * count + rise
    blocks = tuple(green_blocks[:, i : i + 1] for i in range(local))
    en_rest = [("en", bit) for bit in range(1, (n_en - 1).bit_length())]
    rest = en_rest + [("kz", bit) for bit in range(2, (n_kz - 1).bit_length())]

    def early(held, ops):
        value, owner = ops
        for step, (axis, bit) in enumerate(rest):
            other = send_bit(value, axis, bit)
            value = keep_bit(value, other, owner, axis, bit)
            if step == 0:
                last, value = lax.optimization_barrier((held[-1], value))
                held = held[:-1] + (last,)
        return held, value

    def late(held, value):
        pieces = [value] + [None] * 3
        for j in (3, 2, 1):
            pieces[j] = flip(value, j // 2 * 2, j % 2)
        return held, tuple(pieces) + (flip(jnp.stack(pieces), 1, 0),)

    blocks, index_first, index_more = lax.optimization_barrier((blocks, index[0], index[1]))
    near, value = move(blocks, index_first, 1, early, (value, owners))
    far, pieces = move(near, index_more, 0, late, value)
    return sandwich_sum(energy_shift, pieces, near + far, green_blocks.shape)


def solution(mesh):
    in_specs = (P("kz", "en", None, None, None), P("kz", "en", None, None, None), P(), P(), P())
    out_specs = P("kz", "en", None, None, None)
    return jax.shard_map(shards, mesh=mesh, in_specs=in_specs, out_specs=out_specs, check_vma=False)
```

time: 94.9 us -> 90.8 us (0.957)
  the two profiles are of different devices: /device:TPU:24 before, /device:TPU:27 now
where the time goes in v1:
time: 90.8 us; the launch traced here: 90.5 us
  starting transfers between devices  41.9 us (46%)
  waiting for transfers between devices  34.4 us (38%)
  Pallas kernels  7.04 us (8%)
  local copies, waits for them, and re-layouts  3.83 us (4%)
  between operations  1.56 us (2%)
  other arithmetic  1.47 us (2%)
    ppermute x10, waiting for transfers between devices, flip(): return lax.ppermute(array, AXES, pairs_flip(kz_bits, en_bits))  34.4 us
    ppermute x10, starting transfers between devices, flip(): return lax.ppermute(array, AXES, pairs_flip(kz_bits, en_bits))  33.7 us
    ppermute x4, starting transfers between devices, shift_blocks(): out.append(lax.ppermute(blocks[source], AXES, pairs_shift(momentum, steps)))  8.21 us
    pallas_call x1, Pallas kernels, sandwich_sum(): pl.pallas_call(kernel, out_shape=jax.ShapeDtypeStruct(shape, jnp.float32)...  7.04 us
    unnamed x10, local copies, waits for them, and re-layouts  1.87 us
  transfers between devices with their start and end apart: 14, of which 8 were waited for; matrix products, arithmetic and copies ran while one was open for 2% of the time, Pallas kernels for 0%

profile of v1, /device:TPU:27, one launch (start us, length us, event | category | flops | bytes accessed | tf_op | source)
XLA Modules:
  0.0 90.5 jit_solution(4539052124827041415)
XLA Ops:
  0.0 1.0 %dynamic-slice_bitcast_fusion = f32[256,256]{1,0:T(8,128)S(1)} fusion(f32[1,1,2,256,256]{4,3,2,1,0:T(8,128)} %param.62, s32[]{:T(128)S(6)} %select_n.487), kind=kLoop, calls=%fused_computation.196 | loop fusion | bytes 524292 | tf_op jit(solution)/shard_map/jit(dynamic_index_in_dim)/squeeze | solution.py:90
  1.0 0.7 collective-permute-start.276
  1.8 0.7 copy-done.2
  2.5 0.6 copy-done.3
  3.2 0.6 copy-done.4
  3.9 0.6 fusion.31
  4.6 0.1 broadcast_select_fusion.56
  4.7 1.3 %collective-permute-start.277 = (f32[2,64,256]{2,1,0:T(8,128)S(1)}, f32[2,64,256]{2,1,0:T(8,128)S(1)}, u32[]{:S(2)}, u32[]{:S(2)}) collective-permute-start(f32[2,64,256]{2,1,0:T(8,128)S(1)} %get-tuple-element.1537), channel_id=1, source_target_pairs={{0,1},{1,0},{2,3},{3,2},{4,5},{5,4},{6,7},{7,6},{8,9},{9,8},{10,11... | collective-permute-start | bytes 393224 | tf_op jit(solution)/shard_map/ppermute | solution.py:34
  6.0 0.3 collective-permute-start.278
  6.2 1.2 %collective-permute-start.279 = (f32[2,64,256]{2,1,0:T(8,128)S(1)}, f32[2,64,256]{2,1,0:T(8,128)S(1)}, u32[]{:S(2)}, u32[]{:S(2)}) collective-permute-start(f32[2,64,256]{2,1,0:T(8,128)S(1)} %get-tuple-element.1540), channel_id=1, source_target_pairs={{0,17},{1,16},{2,19},{3,18},{4,21},{5,20},{6,23},{7,22},{8,25},{9,... | collective-permute-start | bytes 393224 | tf_op jit(solution)/shard_map/ppermute | solution.py:34
  8.8 0.9 %collective-permute-done.277 = f32[2,64,256]{2,1,0:T(8,128)S(1)} collective-permute-done((f32[2,64,256]{2,1,0:T(8,128)S(1)}, f32[2,64,256]{2,1,0:T(8,128)S(1)}, u32[]{:S(2)}, u32[]{:S(2)}) %collective-permute-start.277) | collective-permute-done | bytes 131104 | tf_op jit(solution)/shard_map/ppermute | solution.py:34
  9.7 1.0 %collective-permute-done.278 = f32[2,64,256]{2,1,0:T(8,128)S(1)} collective-permute-done((f32[2,64,256]{2,1,0:T(8,128)S(1)}, f32[2,64,256]{2,1,0:T(8,128)S(1)}, u32[]{:S(2)}, u32[]{:S(2)}) %collective-permute-start.278) | collective-permute-done | bytes 131104 | tf_op jit(solution)/shard_map/ppermute | solution.py:34
  10.7 2.8 %collective-permute-done.279 = f32[2,64,256]{2,1,0:T(8,128)S(1)} collective-permute-done((f32[2,64,256]{2,1,0:T(8,128)S(1)}, f32[2,64,256]{2,1,0:T(8,128)S(1)}, u32[]{:S(2)}, u32[]{:S(2)}) %collective-permute-start.279) | collective-permute-done | bytes 131104 | tf_op jit(solution)/shard_map/ppermute | solution.py:34
  13.4 34.7 %conditional.2 = (f32[1,1,2,256,256]{4,3,2,1,0:T(8,128)}, f32[1,1,2,256,256]{4,3,2,1,0:T(8,128)}, f32[2,64,256]{2,1,0:T(8,128)S(1)}) conditional(s32[]{:T(128)} %clamp.46, (s32[2]{0:T(128)S(1)}, s32[2]{0:T(128)S(1)}, s32[2]{0:T(128)S(1)}, s32[2]{0:T(128)S(1)}, f32[2,64,256]{2,1,0:T(8,128)S(1)}, ...), branch_computations={%region_0.1_spmd, %region_1.2_spmd, %region_2.3_spmd, %region_3.4_... | conditional | flops 163864 | bytes 6684984 | solution.py:62
  13.6 0.2 collective-permute-start.261
  13.8 1.3 %collective-permute-start.260 = (f32[1,1,2,256,256]{4,3,2,1,0:T(8,128)S(1)}, f32[1,1,2,256,256]{4,3,2,1,0:T(8,128)}, u32[]{:S(2)}, u32[]{:S(2)}) collective-permute-start(f32[1,1,2,256,256]{4,3,2,1,0:T(8,128)S(1)} %get-tuple-element.1385), channel_id=1, source_target_pairs={{0,26},{1,27},{2,28},{3,29},{4,30},{5,31},{8,2},{9,3},{10,4},{11,5... | collective-permute-start | bytes 1572872 | tf_op jit(solution)/shard_map/cond/branch_24_fun/ppermute | solution.py:46
  15.1 2.3 %collective-permute-done.261 = f32[2,64,256]{2,1,0:T(8,128)S(1)} collective-permute-done((f32[2,64,256]{2,1,0:T(8,128)S(1)}, f32[2,64,256]{2,1,0:T(8,128)S(1)}, u32[]{:S(2)}, u32[]{:S(2)}) %collective-permute-start.261) | collective-permute-done | bytes 131104 | tf_op jit(solution)/shard_map/cond/branch_24_fun/ppermute | solution.py:34
  17.5 1.3 %collective-permute-start.262 = (f32[1,1,2,256,256]{4,3,2,1,0:T(8,128)S(1)}, f32[1,1,2,256,256]{4,3,2,1,0:T(8,128)}, u32[]{:S(2)}, u32[]{:S(2)}) collective-permute-start(f32[1,1,2,256,256]{4,3,2,1,0:T(8,128)S(1)} %get-tuple-element.1395), channel_id=1, source_target_pairs={{0,26},{1,27},{2,28},{3,29},{4,30},{5,31},{8,2},{9,3},{10,4},{11,5... | collective-permute-start | bytes 1572872 | tf_op jit(solution)/shard_map/cond/branch_24_fun/ppermute | solution.py:46
  18.8 4.3 %collective-permute-start.263 = (f32[2,64,256]{2,1,0:T(8,128)S(1)}, f32[2,64,256]{2,1,0:T(8,128)S(1)}, u32[]{:S(2)}, u32[]{:S(2)}) collective-permute-start(f32[2,64,256]{2,1,0:T(8,128)S(1)} %broadcast_select_fusion.49), channel_id=1, source_target_pairs={{0,4},{1,5},{2,6},{3,7},{4,0},{5,1},{6,2},{7,3},{8,12},{9,13},{10,... | collective-permute-start | bytes 393224 | tf_op jit(solution)/shard_map/cond/branch_24_fun/ppermute | solution.py:34
  23.1 24.8 %collective-permute-done.263 = f32[2,64,256]{2,1,0:T(8,128)S(1)} collective-permute-done((f32[2,64,256]{2,1,0:T(8,128)S(1)}, f32[2,64,256]{2,1,0:T(8,128)S(1)}, u32[]{:S(2)}, u32[]{:S(2)}) %collective-permute-start.263) | collective-permute-done | bytes 131104 | tf_op jit(solution)/shard_map/cond/branch_24_fun/ppermute | solution.py:34
  48.2 35.1 %conditional.3 = (f32[1,1,2,256,256]{4,3,2,1,0:T(8,128)}, f32[1,1,2,256,256]{4,3,2,1,0:T(8,128)}, f32[2,64,256]{2,1,0:T(8,128)}, f32[2,64,256]{2,1,0:T(8,128)}, ...) conditional(s32[]{:T(128)} %clamp.47, (f32[2,64,256]{2,1,0:T(8,128)S(1)}, ...), branch_computations={%region_28.29_spmd, %region_29.30_spmd, %region_30.31_spmd, %regio... | conditional | flops 393216 | bytes 8913184 | solution.py:62
  48.3 2.1 %collective-permute-start.139 = (f32[2,64,256]{2,1,0:T(8,128)S(1)}, f32[2,64,256]{2,1,0:T(8,128)}, u32[]{:S(2)}, u32[]{:S(2)}) collective-permute-start(f32[2,64,256]{2,1,0:T(8,128)S(1)} %get-tuple-element.1504), channel_id=1, source_target_pairs={{0,17},{1,16},{2,19},{3,18},{4,21},{5,20},{6,23},{7,22},{8,25},{9,... | collective-permute-start | bytes 393224 | tf_op jit(solution)/shard_map/cond/branch_23_fun/ppermute | solution.py:34
  50.4 0.2 collective-permute-start.138
  50.6 0.4 collective-permute-start.137
  51.0 3.7 %collective-permute-start.135 = (f32[1,1,2,256,256]{4,3,2,1,0:T(8,128)}, f32[1,1,2,256,256]{4,3,2,1,0:T(8,128)}, u32[]{:S(2)}, u32[]{:S(2)}) collective-permute-start(f32[1,1,2,256,256]{4,3,2,1,0:T(8,128)} %get-tuple-element.1502), channel_id=1, source_target_pairs={{0,25},{1,26},{2,27},{3,28},{4,29},{5,30},{6,31},{8,1},{9,2},{10,3... | collective-permute-start | bytes 1572872 | tf_op jit(solution)/shard_map/cond/branch_23_fun/ppermute | solution.py:46
  54.7 1.9 %collective-permute-start.136 = (f32[1,1,2,256,256]{4,3,2,1,0:T(8,128)}, f32[1,1,2,256,256]{4,3,2,1,0:T(8,128)}, u32[]{:S(2)}, u32[]{:S(2)}) collective-permute-start(f32[1,1,2,256,256]{4,3,2,1,0:T(8,128)} %get-tuple-element.1503), channel_id=1, source_target_pairs={{0,25},{1,26},{2,27},{3,28},{4,29},{5,30},{6,31},{8,1},{9,2},{10,3... | collective-permute-start | bytes 1572872 | tf_op jit(solution)/shard_map/cond/branch_23_fun/ppermute | solution.py:46
  56.6 0.6 collective-permute-done.138
  57.3 0.3 collective-permute-done.137
  57.6 1.1 %pad_maximum_fusion.23 = f32[4,2,64,256]{3,2,1,0:T(8,128)S(1)} fusion(f32[1,2,64,256]{3,2,1,0:T(8,128)} %bitcast.95, f32[1,2,64,256]{3,2,1,0:T(8,128)} %bitcast.94, f32[1,2,64,256]{3,2,1,0:T(8,128)} %bitcast.93, f32[1,2,64,256]{3,2,1,0:T(8,128)S(1)} %bitcast.147), kind=kLoop, calls=%fused_computation.191 | loop fusion | flops 393216 | bytes 1048576 | tf_op jit(solution)/shard_map/cond/branch_23_fun/stack | solution.py:257
  58.6 23.0 %collective-permute-start.140 = (f32[4,2,64,256]{3,2,1,0:T(8,128)S(1)}, f32[4,2,64,256]{3,2,1,0:T(8,128)}, u32[]{:S(2)}, u32[]{:S(2)}) collective-permute-start(f32[4,2,64,256]{3,2,1,0:T(8,128)S(1)} %pad_maximum_fusion.23), channel_id=1, source_target_pairs={{0,8},{1,9},{2,10},{3,11},{4,12},{5,13},{6,14},{7,15},{8,0},{9,1},... | collective-permute-start | bytes 1572872 | tf_op jit(solution)/shard_map/cond/branch_23_fun/ppermute | solution.py:34
  81.6 1.7 %collective-permute-done.140 = f32[4,2,64,256]{3,2,1,0:T(8,128)} collective-permute-done((f32[4,2,64,256]{3,2,1,0:T(8,128)S(1)}, f32[4,2,64,256]{3,2,1,0:T(8,128)}, u32[]{:S(2)}, u32[]{:S(2)}) %collective-permute-start.140) | collective-permute-done | bytes 524320 | tf_op jit(solution)/shard_map/cond/branch_23_fun/ppermute | solution.py:34
  83.3 7.0 %sandwich_sum.1 = f32[1,2,2,256,256]{4,3,2,1,0:T(8,128)} custom-call(s32[2]{0:T(128)} %energy.1, f32[2,64,256]{2,1,0:T(8,128)S(1)} %get-tuple-element.1543.refs_0_, f32[2,64,256]{2,1,0:T(8,128)} %get-tuple-element.1547.refs_1_, f32[2,64,256]{2,1,0:T(8,128)} %get-tuple-element.1548.refs_2_, f32[2,64,256]{2,1,0:T(8,128)} %get-tuple-element.1549.refs_3_, ...), custom_call_target="tpu_custom_call" | custom-call | flops 2415919104 | bytes 4194304 | tf_op jit(solution)/shard_map/sandwich_sum/pallas_call | solution.py:203
  (28 shorter events, 0.7 us)
Async XLA Ops:
  0.0 3.9 %copy-start.1 = (f32[1,1,2,256,256]{4,3,2,1,0:T(8,128)S(1)}, f32[1,1,2,256,256]{4,3,2,1,0:T(8,128)}, u32[]{:S(2)}) copy-start(f32[1,1,2,256,256]{4,3,2,1,0:T(8,128)} %param.62) | copy-start | bytes 1572868
  1.0 3.5 %collective-permute-start.276 = (f32[256,256]{1,0:T(8,128)S(1)}, f32[256,256]{1,0:T(8,128)S(1)}, u32[]{:S(2)}, u32[]{:S(2)}) collective-permute-start(f32[256,256]{1,0:T(8,128)S(1)} %dynamic-slice_bitcast_fusion), channel_id=1, source_target_pairs={{0,8},{1,9},{2,10},{3,11},{4,12},{5,13},{6,14},{7,15},{8,0},{9,1},... | collective-permute-start | bytes 786440 | tf_op jit(solution)/shard_map/ppermute | solution.py:34
  1.8 0.7 copy-start.2
  2.4 0.7 copy-start.3
  3.1 0.7 copy-start.4
  3.9 3.5 %copy-start = (f32[1,2,2,256,256]{4,3,2,1,0:T(8,128)S(1)}, f32[1,2,2,256,256]{4,3,2,1,0:T(8,128)}, u32[]{:S(2)}) copy-start(f32[1,2,2,256,256]{4,3,2,1,0:T(8,128)} %param.61) | copy-start | bytes 3145732
  4.7 5.1 %collective-permute-start.277 = (f32[2,64,256]{2,1,0:T(8,128)S(1)}, f32[2,64,256]{2,1,0:T(8,128)S(1)}, u32[]{:S(2)}, u32[]{:S(2)}) collective-permute-start(f32[2,64,256]{2,1,0:T(8,128)S(1)} %get-tuple-element.1537), channel_id=1, source_target_pairs={{0,1},{1,0},{2,3},{3,2},{4,5},{5,4},{6,7},{7,6},{8,9},{9,8},{10,11... | collective-permute-start | bytes 393224 | tf_op jit(solution)/shard_map/ppermute | solution.py:34
  6.0 4.7 %collective-permute-start.278 = (f32[2,64,256]{2,1,0:T(8,128)S(1)}, f32[2,64,256]{2,1,0:T(8,128)S(1)}, u32[]{:S(2)}, u32[]{:S(2)}) collective-permute-start(f32[2,64,256]{2,1,0:T(8,128)S(1)} %get-tuple-element.1539), channel_id=1, source_target_pairs={{0,16},{1,17},{2,18},{3,19},{4,20},{5,21},{6,22},{7,23},{8,24},{9,... | collective-permute-start | bytes 393224 | tf_op jit(solution)/shard_map/ppermute | solution.py:34
  6.2 7.2 %collective-permute-start.279 = (f32[2,64,256]{2,1,0:T(8,128)S(1)}, f32[2,64,256]{2,1,0:T(8,128)S(1)}, u32[]{:S(2)}, u32[]{:S(2)}) collective-permute-start(f32[2,64,256]{2,1,0:T(8,128)S(1)} %get-tuple-element.1540), channel_id=1, source_target_pairs={{0,17},{1,16},{2,19},{3,18},{4,21},{5,20},{6,23},{7,22},{8,25},{9,... | collective-permute-start | bytes 393224 | tf_op jit(solution)/shard_map/ppermute | solution.py:34
  13.6 3.9 %collective-permute-start.261 = (f32[2,64,256]{2,1,0:T(8,128)S(1)}, f32[2,64,256]{2,1,0:T(8,128)S(1)}, u32[]{:S(2)}, u32[]{:S(2)}) collective-permute-start(f32[2,64,256]{2,1,0:T(8,128)S(1)} %select_select_fusion.24), channel_id=1, source_target_pairs={{0,2},{1,3},{2,0},{3,1},{4,6},{5,7},{6,4},{7,5},{8,10},{9,11},{10,... | collective-permute-start | bytes 393224 | tf_op jit(solution)/shard_map/cond/branch_24_fun/ppermute | solution.py:34
  13.8 34.2 %collective-permute-start.260 = (f32[1,1,2,256,256]{4,3,2,1,0:T(8,128)S(1)}, f32[1,1,2,256,256]{4,3,2,1,0:T(8,128)}, u32[]{:S(2)}, u32[]{:S(2)}) collective-permute-start(f32[1,1,2,256,256]{4,3,2,1,0:T(8,128)S(1)} %get-tuple-element.1385), channel_id=1, source_target_pairs={{0,26},{1,27},{2,28},{3,29},{4,30},{5,31},{8,2},{9,3},{10,4},{11,5... | collective-permute-start | bytes 1572872 | tf_op jit(solution)/shard_map/cond/branch_24_fun/ppermute | solution.py:46
  17.5 30.5 %collective-permute-start.262 = (f32[1,1,2,256,256]{4,3,2,1,0:T(8,128)S(1)}, f32[1,1,2,256,256]{4,3,2,1,0:T(8,128)}, u32[]{:S(2)}, u32[]{:S(2)}) collective-permute-start(f32[1,1,2,256,256]{4,3,2,1,0:T(8,128)S(1)} %get-tuple-element.1395), channel_id=1, source_target_pairs={{0,26},{1,27},{2,28},{3,29},{4,30},{5,31},{8,2},{9,3},{10,4},{11,5... | collective-permute-start | bytes 1572872 | tf_op jit(solution)/shard_map/cond/branch_24_fun/ppermute | solution.py:46
  18.8 29.1 %collective-permute-start.263 = (f32[2,64,256]{2,1,0:T(8,128)S(1)}, f32[2,64,256]{2,1,0:T(8,128)S(1)}, u32[]{:S(2)}, u32[]{:S(2)}) collective-permute-start(f32[2,64,256]{2,1,0:T(8,128)S(1)} %broadcast_select_fusion.49), channel_id=1, source_target_pairs={{0,4},{1,5},{2,6},{3,7},{4,0},{5,1},{6,2},{7,3},{8,12},{9,13},{10,... | collective-permute-start | bytes 393224 | tf_op jit(solution)/shard_map/cond/branch_24_fun/ppermute | solution.py:34
  48.3 8.4 %collective-permute-start.139 = (f32[2,64,256]{2,1,0:T(8,128)S(1)}, f32[2,64,256]{2,1,0:T(8,128)}, u32[]{:S(2)}, u32[]{:S(2)}) collective-permute-start(f32[2,64,256]{2,1,0:T(8,128)S(1)} %get-tuple-element.1504), channel_id=1, source_target_pairs={{0,17},{1,16},{2,19},{3,18},{4,21},{5,20},{6,23},{7,22},{8,25},{9,... | collective-permute-start | bytes 393224 | tf_op jit(solution)/shard_map/cond/branch_23_fun/ppermute | solution.py:34
  50.4 6.9 %collective-permute-start.138 = (f32[2,64,256]{2,1,0:T(8,128)S(1)}, f32[2,64,256]{2,1,0:T(8,128)}, u32[]{:S(2)}, u32[]{:S(2)}) collective-permute-start(f32[2,64,256]{2,1,0:T(8,128)S(1)} %get-tuple-element.1504), channel_id=1, source_target_pairs={{0,16},{1,17},{2,18},{3,19},{4,20},{5,21},{6,22},{7,23},{8,24},{9,... | collective-permute-start | bytes 393224 | tf_op jit(solution)/shard_map/cond/branch_23_fun/ppermute | solution.py:34
  50.6 7.0 %collective-permute-start.137 = (f32[2,64,256]{2,1,0:T(8,128)S(1)}, f32[2,64,256]{2,1,0:T(8,128)}, u32[]{:S(2)}, u32[]{:S(2)}) collective-permute-start(f32[2,64,256]{2,1,0:T(8,128)S(1)} %get-tuple-element.1504), channel_id=1, source_target_pairs={{0,1},{1,0},{2,3},{3,2},{4,5},{5,4},{6,7},{7,6},{8,9},{9,8},{10,11... | collective-permute-start | bytes 393224 | tf_op jit(solution)/shard_map/cond/branch_23_fun/ppermute | solution.py:34
  51.0 30.6 %collective-permute-start.135 = (f32[1,1,2,256,256]{4,3,2,1,0:T(8,128)}, f32[1,1,2,256,256]{4,3,2,1,0:T(8,128)}, u32[]{:S(2)}, u32[]{:S(2)}) collective-permute-start(f32[1,1,2,256,256]{4,3,2,1,0:T(8,128)} %get-tuple-element.1502), channel_id=1, source_target_pairs={{0,25},{1,26},{2,27},{3,28},{4,29},{5,30},{6,31},{8,1},{9,2},{10,3... | collective-permute-start | bytes 1572872 | tf_op jit(solution)/shard_map/cond/branch_23_fun/ppermute | solution.py:46
  54.7 26.9 %collective-permute-start.136 = (f32[1,1,2,256,256]{4,3,2,1,0:T(8,128)}, f32[1,1,2,256,256]{4,3,2,1,0:T(8,128)}, u32[]{:S(2)}, u32[]{:S(2)}) collective-permute-start(f32[1,1,2,256,256]{4,3,2,1,0:T(8,128)} %get-tuple-element.1503), channel_id=1, source_target_pairs={{0,25},{1,26},{2,27},{3,28},{4,29},{5,30},{6,31},{8,1},{9,2},{10,3... | collective-permute-start | bytes 1572872 | tf_op jit(solution)/shard_map/cond/branch_23_fun/ppermute | solution.py:46
  58.6 24.6 %collective-permute-start.140 = (f32[4,2,64,256]{3,2,1,0:T(8,128)S(1)}, f32[4,2,64,256]{3,2,1,0:T(8,128)}, u32[]{:S(2)}, u32[]{:S(2)}) collective-permute-start(f32[4,2,64,256]{3,2,1,0:T(8,128)S(1)} %pad_maximum_fusion.23), channel_id=1, source_target_pairs={{0,8},{1,9},{2,10},{3,11},{4,12},{5,13},{6,14},{7,15},{8,0},{9,1},... | collective-permute-start | bytes 1572872 | tf_op jit(solution)/shard_map/cond/branch_23_fun/ppermute | solution.py:34

commit v2 on v1

--- a/solution.py
+++ b/solution.py
@@ -18,10 +18,7 @@
 def pairs_shift(momentum, energy):
     n_kz, n_en = sizes()
     return [
-        (k * n_en + d, (k + momentum) % n_kz * n_en + d + energy)
-        for k in range(n_kz)
-        for d in range(n_en)
-        if d + energy < n_en
+        (k * n_en + d, (k + momentum) % n_kz * n_en + (d + energy) % n_en) for k in range(n_kz) for d in range(n_en)
     ]
 
 
@@ -146,10 +143,8 @@
     loads.append(pltpu.make_async_copy(near[4], coupling.at[1], sems.at[4]))
     for load in loads:
         load.start()
-    for local in range(2):
-        for mode in range(2):
-            place = local * 2 + mode
-            pltpu.make_async_copy(blocks[mode * 2 + local].at[0, 0], green.at[place], block_sems.at[place]).start()
+    for place in range(4):
+        pltpu.make_async_copy(blocks[place].at[0, 0], green.at[place], block_sems.at[place]).start()
     sums[...] = jnp.zeros_like(sums)
     for load in loads:
         load.wait()
@@ -172,29 +167,44 @@
         top, rest = split(value)
         return dot_nt(jnp.concatenate([top, rest, top], axis=1), cut[mode, which])
 
-    def step(place, _):
-        local, mode = place // 2, place % 2
-        pltpu.make_async_copy(blocks[0].at[0, 0], green.at[place], block_sems.at[place]).wait()
-        real, imag = green[place, 0], green[place, 1]
+    lowest, highest = jnp.minimum(energy[0], energy[1]), jnp.maximum(energy[0], energy[1])
+    base = lax.axis_index("en") * 2
+
+    def step(mode, _):
+        shift = jnp.where(mode == 0, lowest, highest)
+        for local in range(2):
+            place = mode * 2 + local
+            pltpu.make_async_copy(blocks[0].at[0, 0], green.at[place], block_sems.at[place]).wait()
+        pl.when(base + 1 >= shift)(lambda: add_term(mode, base >= shift))
+        return 0
+
+    def add_term(mode, lower):
+        def pair(part):
+            below = jnp.where(lower, green[mode * 2, part], 0.0)
+            return jnp.concatenate([below, green[mode * 2 + 1, part]], axis=1)
+
+        real, imag = pair(0), pair(1)
         first = left(mode, 0, real)
         second = left(mode, 1, imag)
         both = left(mode, 2, real + imag)
-        real, imag = first - second, both - first - second
+        real, imag = stacked(first - second), stacked(both - first - second)
         first = right(mode, 0, real)
         second = right(mode, 1, imag)
-        sums[local, 0] += first + second
-        sums[local, 1] += first - second
-        sums[local, 1] += right(mode, 2, imag - real)
-
-        @pl.when(mode == 1)
-        def _():
-            pltpu.make_async_copy(sums.at[local], out.at[0, local], out_sems.at[local]).start()
-
-        return 0
-
-    lax.fori_loop(0, 4, step, 0)
-    for local in range(2):
-        pltpu.make_async_copy(sums.at[local], out.at[0, local], out_sems.at[local]).wait()
+        add(0, first + second)
+        add(1, first - second)
+        add(1, right(mode, 2, imag - real))
+
+    def stacked(value):
+        return jnp.concatenate([value[:, :size], value[:, size:]], axis=0)
+
+    def add(part, value):
+        for local in range(2):
+            sums[local, part] += value[local * size : (local + 1) * size]
+
+    lax.fori_loop(0, 2, step, 0)
+    store = pltpu.make_async_copy(sums, out.at[0], out_sems.at[0])
+    store.start()
+    store.wait()
 
 
 def sandwich_sum(energy, pieces, blocks, shape):

time: 90.8 us -> 89.6 us (0.987)
  the two profiles are of different devices: /device:TPU:27 before, /device:TPU:25 now
where the time goes in v2:
time: 89.6 us; the launch traced here: 89.3 us
  waiting for transfers between devices  56.5 us (63%)
  starting transfers between devices  18.8 us (21%)
  Pallas kernels  6.66 us (7%)
  local copies, waits for them, and re-layouts  3.83 us (4%)
  between operations  1.6 us (2%)
  other arithmetic  1.47 us (2%)
    ppermute x10, waiting for transfers between devices, flip(): return lax.ppermute(array, AXES, pairs_flip(kz_bits, en_bits))  56.5 us
    ppermute x4, starting transfers between devices, shift_blocks(): out.append(lax.ppermute(blocks[source], AXES, pairs_shift(momentum, steps)))  9.74 us
    ppermute x10, starting transfers between devices, flip(): return lax.ppermute(array, AXES, pairs_flip(kz_bits, en_bits))  9.03 us
    pallas_call x1, Pallas kernels, sandwich_sum(): pl.pallas_call(kernel, out_shape=jax.ShapeDtypeStruct(shape, jnp.float32)...  6.66 us
    unnamed x10, local copies, waits for them, and re-layouts  1.87 us
  transfers between devices with their start and end apart: 14, of which 8 were waited for; matrix products, arithmetic and copies ran while one was open for 2% of the time, Pallas kernels for 0%

profile of v2, /device:TPU:25, one launch (start us, length us, event | category | flops | bytes accessed | tf_op | source)
XLA Modules:
  0.0 89.3 jit_solution(8032361925692484439)
XLA Ops:
  0.0 1.0 %dynamic-slice_bitcast_fusion = f32[256,256]{1,0:T(8,128)S(1)} fusion(f32[1,1,2,256,256]{4,3,2,1,0:T(8,128)} %param.62, s32[]{:T(128)S(6)} %select_n.487), kind=kLoop, calls=%fused_computation.196 | loop fusion | bytes 524292 | tf_op jit(solution)/shard_map/jit(dynamic_index_in_dim)/squeeze | solution.py:87
  1.0 0.7 collective-permute-start.276
  1.8 0.7 copy-done.2
  2.5 0.6 copy-done.3
  3.2 0.6 copy-done.4
  3.9 0.6 fusion.31
  4.6 0.1 broadcast_select_fusion.56
  4.7 1.3 %collective-permute-start.277 = (f32[2,64,256]{2,1,0:T(8,128)S(1)}, f32[2,64,256]{2,1,0:T(8,128)S(1)}, u32[]{:S(2)}, u32[]{:S(2)}) collective-permute-start(f32[2,64,256]{2,1,0:T(8,128)S(1)} %get-tuple-element.1537), channel_id=1, source_target_pairs={{0,1},{1,0},{2,3},{3,2},{4,5},{5,4},{6,7},{7,6},{8,9},{9,8},{10,11... | collective-permute-start | bytes 393224 | tf_op jit(solution)/shard_map/ppermute | solution.py:31
  6.0 1.2 %collective-permute-start.278 = (f32[2,64,256]{2,1,0:T(8,128)S(1)}, f32[2,64,256]{2,1,0:T(8,128)S(1)}, u32[]{:S(2)}, u32[]{:S(2)}) collective-permute-start(f32[2,64,256]{2,1,0:T(8,128)S(1)} %get-tuple-element.1539), channel_id=1, source_target_pairs={{0,16},{1,17},{2,18},{3,19},{4,20},{5,21},{6,22},{7,23},{8,24},{9,... | collective-permute-start | bytes 393224 | tf_op jit(solution)/shard_map/ppermute | solution.py:31
  7.2 0.2 collective-permute-start.279
  8.8 0.9 %collective-permute-done.277 = f32[2,64,256]{2,1,0:T(8,128)S(1)} collective-permute-done((f32[2,64,256]{2,1,0:T(8,128)S(1)}, f32[2,64,256]{2,1,0:T(8,128)S(1)}, u32[]{:S(2)}, u32[]{:S(2)}) %collective-permute-start.277) | collective-permute-done | bytes 131104 | tf_op jit(solution)/shard_map/ppermute | solution.py:31
  9.7 1.0 %collective-permute-done.278 = f32[2,64,256]{2,1,0:T(8,128)S(1)} collective-permute-done((f32[2,64,256]{2,1,0:T(8,128)S(1)}, f32[2,64,256]{2,1,0:T(8,128)S(1)}, u32[]{:S(2)}, u32[]{:S(2)}) %collective-permute-start.278) | collective-permute-done | bytes 131104 | tf_op jit(solution)/shard_map/ppermute | solution.py:31
  10.7 2.9 %collective-permute-done.279 = f32[2,64,256]{2,1,0:T(8,128)S(1)} collective-permute-done((f32[2,64,256]{2,1,0:T(8,128)S(1)}, f32[2,64,256]{2,1,0:T(8,128)S(1)}, u32[]{:S(2)}, u32[]{:S(2)}) %collective-permute-start.279) | collective-permute-done | bytes 131104 | tf_op jit(solution)/shard_map/ppermute | solution.py:31
  13.6 33.5 %conditional.2 = (f32[1,1,2,256,256]{4,3,2,1,0:T(8,128)}, f32[1,1,2,256,256]{4,3,2,1,0:T(8,128)}, f32[2,64,256]{2,1,0:T(8,128)S(1)}) conditional(s32[]{:T(128)} %clamp.46, (s32[2]{0:T(128)S(1)}, s32[2]{0:T(128)S(1)}, s32[2]{0:T(128)S(1)}, s32[2]{0:T(128)S(1)}, f32[2,64,256]{2,1,0:T(8,128)S(1)}, ...), branch_computations={%region_0.1_spmd, %region_1.2_spmd, %region_2.3_spmd, %region_3.4_... | conditional | flops 163864 | bytes 6684984 | solution.py:59
  13.7 0.2 collective-permute-start.261
  14.0 2.3 %collective-permute-start.260 = (f32[1,1,2,256,256]{4,3,2,1,0:T(8,128)S(1)}, f32[1,1,2,256,256]{4,3,2,1,0:T(8,128)}, u32[]{:S(2)}, u32[]{:S(2)}) collective-permute-start(f32[1,1,2,256,256]{4,3,2,1,0:T(8,128)S(1)} %get-tuple-element.1385), channel_id=1, source_target_pairs={{0,26},{1,27},{2,28},{3,29},{4,30},{5,31},{6,24},{7,25},{8,2},{9,3... | collective-permute-start | bytes 1572872 | tf_op jit(solution)/shard_map/cond/branch_24_fun/ppermute | solution.py:43
  16.2 1.4 %collective-permute-done.261 = f32[2,64,256]{2,1,0:T(8,128)S(1)} collective-permute-done((f32[2,64,256]{2,1,0:T(8,128)S(1)}, f32[2,64,256]{2,1,0:T(8,128)S(1)}, u32[]{:S(2)}, u32[]{:S(2)}) %collective-permute-start.261) | collective-permute-done | bytes 131104 | tf_op jit(solution)/shard_map/cond/branch_24_fun/ppermute | solution.py:31
  17.7 2.6 %collective-permute-start.262 = (f32[1,1,2,256,256]{4,3,2,1,0:T(8,128)S(1)}, f32[1,1,2,256,256]{4,3,2,1,0:T(8,128)}, u32[]{:S(2)}, u32[]{:S(2)}) collective-permute-start(f32[1,1,2,256,256]{4,3,2,1,0:T(8,128)S(1)} %get-tuple-element.1395), channel_id=1, source_target_pairs={{0,26},{1,27},{2,28},{3,29},{4,30},{5,31},{6,24},{7,25},{8,2},{9,3... | collective-permute-start | bytes 1572872 | tf_op jit(solution)/shard_map/cond/branch_24_fun/ppermute | solution.py:43
  20.2 1.5 %collective-permute-start.263 = (f32[2,64,256]{2,1,0:T(8,128)S(1)}, f32[2,64,256]{2,1,0:T(8,128)S(1)}, u32[]{:S(2)}, u32[]{:S(2)}) collective-permute-start(f32[2,64,256]{2,1,0:T(8,128)S(1)} %broadcast_select_fusion.49), channel_id=1, source_target_pairs={{0,4},{1,5},{2,6},{3,7},{4,0},{5,1},{6,2},{7,3},{8,12},{9,13},{10,... | collective-permute-start | bytes 393224 | tf_op jit(solution)/shard_map/cond/branch_24_fun/ppermute | solution.py:31
  21.8 25.0 %collective-permute-done.263 = f32[2,64,256]{2,1,0:T(8,128)S(1)} collective-permute-done((f32[2,64,256]{2,1,0:T(8,128)S(1)}, f32[2,64,256]{2,1,0:T(8,128)S(1)}, u32[]{:S(2)}, u32[]{:S(2)}) %collective-permute-start.263) | collective-permute-done | bytes 131104 | tf_op jit(solution)/shard_map/cond/branch_24_fun/ppermute | solution.py:31
  47.1 35.4 %conditional.3 = (f32[1,1,2,256,256]{4,3,2,1,0:T(8,128)}, f32[1,1,2,256,256]{4,3,2,1,0:T(8,128)}, f32[2,64,256]{2,1,0:T(8,128)}, f32[2,64,256]{2,1,0:T(8,128)}, ...) conditional(s32[]{:T(128)} %clamp.47, (f32[2,64,256]{2,1,0:T(8,128)S(1)}, ...), branch_computations={%region_28.29_spmd, %region_29.30_spmd, %region_30.31_spmd, %regio... | conditional | flops 393216 | bytes 8913184 | solution.py:59
  47.4 1.3 %collective-permute-start.139 = (f32[2,64,256]{2,1,0:T(8,128)S(1)}, f32[2,64,256]{2,1,0:T(8,128)}, u32[]{:S(2)}, u32[]{:S(2)}) collective-permute-start(f32[2,64,256]{2,1,0:T(8,128)S(1)} %get-tuple-element.1504), channel_id=1, source_target_pairs={{0,17},{1,16},{2,19},{3,18},{4,21},{5,20},{6,23},{7,22},{8,25},{9,... | collective-permute-start | bytes 393224 | tf_op jit(solution)/shard_map/cond/branch_23_fun/ppermute | solution.py:31
  48.7 1.2 %collective-permute-start.138 = (f32[2,64,256]{2,1,0:T(8,128)S(1)}, f32[2,64,256]{2,1,0:T(8,128)}, u32[]{:S(2)}, u32[]{:S(2)}) collective-permute-start(f32[2,64,256]{2,1,0:T(8,128)S(1)} %get-tuple-element.1504), channel_id=1, source_target_pairs={{0,16},{1,17},{2,18},{3,19},{4,20},{5,21},{6,22},{7,23},{8,24},{9,... | collective-permute-start | bytes 393224 | tf_op jit(solution)/shard_map/cond/branch_23_fun/ppermute | solution.py:31
  49.9 0.2 collective-permute-start.137
  50.1 2.5 %collective-permute-start.135 = (f32[1,1,2,256,256]{4,3,2,1,0:T(8,128)}, f32[1,1,2,256,256]{4,3,2,1,0:T(8,128)}, u32[]{:S(2)}, u32[]{:S(2)}) collective-permute-start(f32[1,1,2,256,256]{4,3,2,1,0:T(8,128)} %get-tuple-element.1502), channel_id=1, source_target_pairs={{0,25},{1,26},{2,27},{3,28},{4,29},{5,30},{6,31},{7,24},{8,1},{9,2... | collective-permute-start | bytes 1572872 | tf_op jit(solution)/shard_map/cond/branch_23_fun/ppermute | solution.py:43
  52.6 2.4 %collective-permute-start.136 = (f32[1,1,2,256,256]{4,3,2,1,0:T(8,128)}, f32[1,1,2,256,256]{4,3,2,1,0:T(8,128)}, u32[]{:S(2)}, u32[]{:S(2)}) collective-permute-start(f32[1,1,2,256,256]{4,3,2,1,0:T(8,128)} %get-tuple-element.1503), channel_id=1, source_target_pairs={{0,25},{1,26},{2,27},{3,28},{4,29},{5,30},{6,31},{7,24},{8,1},{9,2... | collective-permute-start | bytes 1572872 | tf_op jit(solution)/shard_map/cond/branch_23_fun/ppermute | solution.py:43
  55.0 0.8 collective-permute-done.138
  55.9 22.8 %collective-permute-done.137 = f32[2,64,256]{2,1,0:T(8,128)} collective-permute-done((f32[2,64,256]{2,1,0:T(8,128)S(1)}, f32[2,64,256]{2,1,0:T(8,128)}, u32[]{:S(2)}, u32[]{:S(2)}) %collective-permute-start.137) | collective-permute-done | bytes 131104 | tf_op jit(solution)/shard_map/cond/branch_23_fun/ppermute | solution.py:31
  78.7 1.1 %pad_maximum_fusion.23 = f32[4,2,64,256]{3,2,1,0:T(8,128)S(1)} fusion(f32[1,2,64,256]{3,2,1,0:T(8,128)} %bitcast.95, f32[1,2,64,256]{3,2,1,0:T(8,128)} %bitcast.94, f32[1,2,64,256]{3,2,1,0:T(8,128)} %bitcast.93, f32[1,2,64,256]{3,2,1,0:T(8,128)S(1)} %bitcast.147), kind=kLoop, calls=%fused_computation.191 | loop fusion | flops 393216 | bytes 1048576 | tf_op jit(solution)/shard_map/cond/branch_23_fun/stack | solution.py:267
  79.7 1.1 %collective-permute-start.140 = (f32[4,2,64,256]{3,2,1,0:T(8,128)S(1)}, f32[4,2,64,256]{3,2,1,0:T(8,128)}, u32[]{:S(2)}, u32[]{:S(2)}) collective-permute-start(f32[4,2,64,256]{3,2,1,0:T(8,128)S(1)} %pad_maximum_fusion.23), channel_id=1, source_target_pairs={{0,8},{1,9},{2,10},{3,11},{4,12},{5,13},{6,14},{7,15},{8,0},{9,1},... | collective-permute-start | bytes 1572872 | tf_op jit(solution)/shard_map/cond/branch_23_fun/ppermute | solution.py:31
  80.8 1.7 %collective-permute-done.140 = f32[4,2,64,256]{3,2,1,0:T(8,128)} collective-permute-done((f32[4,2,64,256]{3,2,1,0:T(8,128)S(1)}, f32[4,2,64,256]{3,2,1,0:T(8,128)}, u32[]{:S(2)}, u32[]{:S(2)}) %collective-permute-start.140) | collective-permute-done | bytes 524320 | tf_op jit(solution)/shard_map/cond/branch_23_fun/ppermute | solution.py:31
  82.5 6.7 %sandwich_sum.1 = f32[1,2,2,256,256]{4,3,2,1,0:T(8,128)} custom-call(s32[2]{0:T(128)} %energy.1, f32[2,64,256]{2,1,0:T(8,128)S(1)} %get-tuple-element.1543.refs_0_, f32[2,64,256]{2,1,0:T(8,128)} %get-tuple-element.1547.refs_1_, f32[2,64,256]{2,1,0:T(8,128)} %get-tuple-element.1548.refs_2_, f32[2,64,256]{2,1,0:T(8,128)} %get-tuple-element.1549.refs_3_, ...), custom_call_target="tpu_custom_call" | custom-call | flops 2415919104 | bytes 4194304 | tf_op jit(solution)/shard_map/sandwich_sum/pallas_call | solution.py:213
  (28 shorter events, 0.7 us)
Async XLA Ops:
  0.0 3.9 %copy-start.1 = (f32[1,1,2,256,256]{4,3,2,1,0:T(8,128)S(1)}, f32[1,1,2,256,256]{4,3,2,1,0:T(8,128)}, u32[]{:S(2)}) copy-start(f32[1,1,2,256,256]{4,3,2,1,0:T(8,128)} %param.62) | copy-start | bytes 1572868
  1.0 3.5 %collective-permute-start.276 = (f32[256,256]{1,0:T(8,128)S(1)}, f32[256,256]{1,0:T(8,128)S(1)}, u32[]{:S(2)}, u32[]{:S(2)}) collective-permute-start(f32[256,256]{1,0:T(8,128)S(1)} %dynamic-slice_bitcast_fusion), channel_id=1, source_target_pairs={{0,8},{1,9},{2,10},{3,11},{4,12},{5,13},{6,14},{7,15},{8,0},{9,1},... | collective-permute-start | bytes 786440 | tf_op jit(solution)/shard_map/ppermute | solution.py:31
  1.8 0.7 copy-start.2
  2.4 0.7 copy-start.3
  3.1 0.7 copy-start.4
  3.9 3.5 %copy-start = (f32[1,2,2,256,256]{4,3,2,1,0:T(8,128)S(1)}, f32[1,2,2,256,256]{4,3,2,1,0:T(8,128)}, u32[]{:S(2)}) copy-start(f32[1,2,2,256,256]{4,3,2,1,0:T(8,128)} %param.61) | copy-start | bytes 3145732
  4.7 5.1 %collective-permute-start.277 = (f32[2,64,256]{2,1,0:T(8,128)S(1)}, f32[2,64,256]{2,1,0:T(8,128)S(1)}, u32[]{:S(2)}, u32[]{:S(2)}) collective-permute-start(f32[2,64,256]{2,1,0:T(8,128)S(1)} %get-tuple-element.1537), channel_id=1, source_target_pairs={{0,1},{1,0},{2,3},{3,2},{4,5},{5,4},{6,7},{7,6},{8,9},{9,8},{10,11... | collective-permute-start | bytes 393224 | tf_op jit(solution)/shard_map/ppermute | solution.py:31
  6.0 4.7 %collective-permute-start.278 = (f32[2,64,256]{2,1,0:T(8,128)S(1)}, f32[2,64,256]{2,1,0:T(8,128)S(1)}, u32[]{:S(2)}, u32[]{:S(2)}) collective-permute-start(f32[2,64,256]{2,1,0:T(8,128)S(1)} %get-tuple-element.1539), channel_id=1, source_target_pairs={{0,16},{1,17},{2,18},{3,19},{4,20},{5,21},{6,22},{7,23},{8,24},{9,... | collective-permute-start | bytes 393224 | tf_op jit(solution)/shard_map/ppermute | solution.py:31
  7.2 6.4 %collective-permute-start.279 = (f32[2,64,256]{2,1,0:T(8,128)S(1)}, f32[2,64,256]{2,1,0:T(8,128)S(1)}, u32[]{:S(2)}, u32[]{:S(2)}) collective-permute-start(f32[2,64,256]{2,1,0:T(8,128)S(1)} %get-tuple-element.1540), channel_id=1, source_target_pairs={{0,17},{1,16},{2,19},{3,18},{4,21},{5,20},{6,23},{7,22},{8,25},{9,... | collective-permute-start | bytes 393224 | tf_op jit(solution)/shard_map/ppermute | solution.py:31
  13.7 3.9 %collective-permute-start.261 = (f32[2,64,256]{2,1,0:T(8,128)S(1)}, f32[2,64,256]{2,1,0:T(8,128)S(1)}, u32[]{:S(2)}, u32[]{:S(2)}) collective-permute-start(f32[2,64,256]{2,1,0:T(8,128)S(1)} %select_select_fusion.24), channel_id=1, source_target_pairs={{0,2},{1,3},{2,0},{3,1},{4,6},{5,7},{6,4},{7,5},{8,10},{9,11},{10,... | collective-permute-start | bytes 393224 | tf_op jit(solution)/shard_map/cond/branch_24_fun/ppermute | solution.py:31
  14.0 33.0 %collective-permute-start.260 = (f32[1,1,2,256,256]{4,3,2,1,0:T(8,128)S(1)}, f32[1,1,2,256,256]{4,3,2,1,0:T(8,128)}, u32[]{:S(2)}, u32[]{:S(2)}) collective-permute-start(f32[1,1,2,256,256]{4,3,2,1,0:T(8,128)S(1)} %get-tuple-element.1385), channel_id=1, source_target_pairs={{0,26},{1,27},{2,28},{3,29},{4,30},{5,31},{6,24},{7,25},{8,2},{9,3... | collective-permute-start | bytes 1572872 | tf_op jit(solution)/shard_map/cond/branch_24_fun/ppermute | solution.py:43
  17.7 29.2 %collective-permute-start.262 = (f32[1,1,2,256,256]{4,3,2,1,0:T(8,128)S(1)}, f32[1,1,2,256,256]{4,3,2,1,0:T(8,128)}, u32[]{:S(2)}, u32[]{:S(2)}) collective-permute-start(f32[1,1,2,256,256]{4,3,2,1,0:T(8,128)S(1)} %get-tuple-element.1395), channel_id=1, source_target_pairs={{0,26},{1,27},{2,28},{3,29},{4,30},{5,31},{6,24},{7,25},{8,2},{9,3... | collective-permute-start | bytes 1572872 | tf_op jit(solution)/shard_map/cond/branch_24_fun/ppermute | solution.py:43
  20.2 26.6 %collective-permute-start.263 = (f32[2,64,256]{2,1,0:T(8,128)S(1)}, f32[2,64,256]{2,1,0:T(8,128)S(1)}, u32[]{:S(2)}, u32[]{:S(2)}) collective-permute-start(f32[2,64,256]{2,1,0:T(8,128)S(1)} %broadcast_select_fusion.49), channel_id=1, source_target_pairs={{0,4},{1,5},{2,6},{3,7},{4,0},{5,1},{6,2},{7,3},{8,12},{9,13},{10,... | collective-permute-start | bytes 393224 | tf_op jit(solution)/shard_map/cond/branch_24_fun/ppermute | solution.py:31
  47.4 7.6 %collective-permute-start.139 = (f32[2,64,256]{2,1,0:T(8,128)S(1)}, f32[2,64,256]{2,1,0:T(8,128)}, u32[]{:S(2)}, u32[]{:S(2)}) collective-permute-start(f32[2,64,256]{2,1,0:T(8,128)S(1)} %get-tuple-element.1504), channel_id=1, source_target_pairs={{0,17},{1,16},{2,19},{3,18},{4,21},{5,20},{6,23},{7,22},{8,25},{9,... | collective-permute-start | bytes 393224 | tf_op jit(solution)/shard_map/cond/branch_23_fun/ppermute | solution.py:31
  48.7 7.2 %collective-permute-start.138 = (f32[2,64,256]{2,1,0:T(8,128)S(1)}, f32[2,64,256]{2,1,0:T(8,128)}, u32[]{:S(2)}, u32[]{:S(2)}) collective-permute-start(f32[2,64,256]{2,1,0:T(8,128)S(1)} %get-tuple-element.1504), channel_id=1, source_target_pairs={{0,16},{1,17},{2,18},{3,19},{4,20},{5,21},{6,22},{7,23},{8,24},{9,... | collective-permute-start | bytes 393224 | tf_op jit(solution)/shard_map/cond/branch_23_fun/ppermute | solution.py:31
  49.9 28.7 %collective-permute-start.137 = (f32[2,64,256]{2,1,0:T(8,128)S(1)}, f32[2,64,256]{2,1,0:T(8,128)}, u32[]{:S(2)}, u32[]{:S(2)}) collective-permute-start(f32[2,64,256]{2,1,0:T(8,128)S(1)} %get-tuple-element.1504), channel_id=1, source_target_pairs={{0,1},{1,0},{2,3},{3,2},{4,5},{5,4},{6,7},{7,6},{8,9},{9,8},{10,11... | collective-permute-start | bytes 393224 | tf_op jit(solution)/shard_map/cond/branch_23_fun/ppermute | solution.py:31
  50.1 30.7 %collective-permute-start.135 = (f32[1,1,2,256,256]{4,3,2,1,0:T(8,128)}, f32[1,1,2,256,256]{4,3,2,1,0:T(8,128)}, u32[]{:S(2)}, u32[]{:S(2)}) collective-permute-start(f32[1,1,2,256,256]{4,3,2,1,0:T(8,128)} %get-tuple-element.1502), channel_id=1, source_target_pairs={{0,25},{1,26},{2,27},{3,28},{4,29},{5,30},{6,31},{7,24},{8,1},{9,2... | collective-permute-start | bytes 1572872 | tf_op jit(solution)/shard_map/cond/branch_23_fun/ppermute | solution.py:43
  52.6 28.2 %collective-permute-start.136 = (f32[1,1,2,256,256]{4,3,2,1,0:T(8,128)}, f32[1,1,2,256,256]{4,3,2,1,0:T(8,128)}, u32[]{:S(2)}, u32[]{:S(2)}) collective-permute-start(f32[1,1,2,256,256]{4,3,2,1,0:T(8,128)} %get-tuple-element.1503), channel_id=1, source_target_pairs={{0,25},{1,26},{2,27},{3,28},{4,29},{5,30},{6,31},{7,24},{8,1},{9,2... | collective-permute-start | bytes 1572872 | tf_op jit(solution)/shard_map/cond/branch_23_fun/ppermute | solution.py:43
  79.7 2.8 %collective-permute-start.140 = (f32[4,2,64,256]{3,2,1,0:T(8,128)S(1)}, f32[4,2,64,256]{3,2,1,0:T(8,128)}, u32[]{:S(2)}, u32[]{:S(2)}) collective-permute-start(f32[4,2,64,256]{3,2,1,0:T(8,128)S(1)} %pad_maximum_fusion.23), channel_id=1, source_target_pairs={{0,8},{1,9},{2,10},{3,11},{4,12},{5,13},{6,14},{7,15},{8,0},{9,1},... | collective-permute-start | bytes 1572872 | tf_op jit(solution)/shard_map/cond/branch_23_fun/ppermute | solution.py:31
